TPU v7x, 256 devices: a whole 4x4x8 slice. The times are simulated.
256 devices in a mesh: trow: 4 (over y), tcol: 4 (over x), pix: 16 (over z, core).
Axes of the slice: x: 4, y: 4, z: 8, core: 2. Of those that a mesh axis runs over, the one named last changes fastest.
Arguments:
- frames: float32 [6144, 2, 64, 128], P(('trow', 'tcol'), None, 'pix'), may hold values from 0.1 to 8
- drift: int32 [6144, 2], P(('trow', 'tcol')), may hold values from -7 to 7
Outputs:
- inner_cycle: float32 [6144, 6144], P(('trow', 'pix'), 'tcol')
- second_band_twotime: float32 [6144, 6144], P(('trow', 'pix'), 'tcol')
All inputs are finite; a program needn't handle non-finite values.
Results may differ from a plain program's by a relative error of at most 0.0003.
Values may be sent and summed in bfloat16 or wider, within the bound.
A program may use at most 128 MiB of HBM per device.

v0:
```python
import jax
import jax.numpy as jnp
from jax import lax
from jax.sharding import PartitionSpec as P


def extended(cells, sides, width):
    for axis, dim in sides:
        count = lax.axis_size(axis)
        ends = count - 1
        head = lax.slice_in_dim(cells, 0, width, axis=dim)
        tail = lax.slice_in_dim(cells, cells.shape[dim] - width, cells.shape[dim], axis=dim)
        cells = jnp.concatenate(
            [
                lax.ppermute(tail, axis, [(i, (i + 1) % count) for i in range(ends)]),
                cells,
                lax.ppermute(head, axis, [((i + 1) % count, i) for i in range(ends)]),
            ],
            axis=dim,
        )
    return cells


def blend(padded, steps, device_axis):
    upward = (jnp.maximum(steps, 0).astype(jnp.float32) / 8.0)[:, None, None, None]
    downward = (jnp.maximum(-steps, 0).astype(jnp.float32) / 8.0)[:, None, None, None]
    length = padded.shape[device_axis] - 2
    middle = lax.slice_in_dim(padded, 1, 1 + length, 1, device_axis)
    after = lax.slice_in_dim(padded, 2, 2 + length, 1, device_axis)
    before = lax.slice_in_dim(padded, 0, length, 1, device_axis)
    return (1.0 - upward - downward) * middle + upward * after + downward * before


def per_device(frames, drift):
    local_frames = frames.shape[0]
    tile_rows = frames.shape[2]
    columns = frames.shape[3]
    total_frames = local_frames * lax.axis_size("trow") * lax.axis_size("tcol")
    band_pixels = tile_rows * columns * lax.axis_size("pix")
    padded = extended(frames.astype(jnp.bfloat16), (("pix", 2),), 1).astype(frames.dtype)
    rowpass = blend(padded, drift[:, 0], 2)
    padded = jnp.pad(rowpass, ((0, 0), (0, 0), (0, 0), (1, 1)))
    shifted = blend(padded, drift[:, 1], 3)
    pixel_mean = lax.psum(jnp.sum(shifted, axis=0), ("trow", "tcol")) / total_frames
    flat = shifted / pixel_mean[None]
    frame_mean = lax.psum(jnp.sum(flat, axis=(2, 3)), "pix") / band_pixels
    normed = (flat / frame_mean[:, :, None, None]).astype(jnp.bfloat16)
    normed = normed.reshape(local_frames, 2, tile_rows * columns)
    block_size = local_frames * lax.axis_size("tcol")
    everything = lax.all_gather(normed, ("trow", "tcol"), axis=0, tiled=True)
    row_frames = lax.dynamic_slice_in_dim(
        everything, lax.axis_index("trow") * block_size, block_size, 0
    )
    col_frames = lax.dynamic_slice_in_dim(
        everything, lax.axis_index("tcol") * block_size, block_size, 0
    )
    own_rows = block_size // lax.axis_size("pix")
    results = []
    for band in range(2):
        band_rows = row_frames[:, band]
        band_cols = col_frames[:, band]

        def partial_gram(start, count, band_rows=band_rows, band_cols=band_cols):
            return lax.dot_general(
                band_rows, band_cols, (((1,), (1,)), ((), ())), preferred_element_type=jnp.float32
            )

        summed = lax.psum_scatter(
            partial_gram(jnp.int32(0), lax.axis_size("pix") * own_rows),
            "pix",
            scatter_dimension=0,
            tiled=True,
        )
        results.append(summed / band_pixels)
    return (results[0], results[1])


def solution(mesh):
    in_specs = (P(("trow", "tcol"), None, "pix", None), P(("trow", "tcol"), None))
    out_specs = (P(("trow", "pix"), "tcol"), P(("trow", "pix"), "tcol"))
    return jax.shard_map(
        per_device, mesh=mesh, in_specs=in_specs, out_specs=out_specs, check_vma=False
    )
```

profile of v0, /device:TPU:6, one launch (start us, length us, event | category | flops | bytes accessed | tf_op | source)
XLA Modules:
  0.0 343.2 jit_solution(5031230959455782191)
XLA Ops:
  7.2 0.0 copy-start
  7.2 0.0 all-gather.2.cloned.1.call-start
  7.2 1.7 copy.10
  9.0 1.8 collective-permute-start
  10.7 1.3 collective-permute-start.1
  12.0 0.0 copy-done
  12.1 0.0 collective-permute-done
  12.1 3.7 %collective-permute-done.1 = bf16[384,2,1,128]{3,0,2,1:T(8,128)(2,1)S(1)} collective-permute-done((bf16[384,2,1,128]{3,0,2,1:T(8,128)(2,1)S(1)}, bf16[384,2,1,128]{3,0,2,1:T(8,128)(2,1)S(1)}, u32[]{:S(2)}, u32[]{:S(2)}) %collective-permute-start.1) | collective-permute-done | bytes 196640 | tf_op jit(solution)/shard_map/ppermute | solution.py:17
  15.8 0.2 maximum_convert_fusion
  15.9 0.4 fusion.6
  16.3 1.0 fusion.11
  17.4 32.7 %psum.14 = f32[2,4,128]{2,1,0:T(4,128)S(1)} all-reduce(f32[2,4,128]{2,1,0:T(4,128)S(1)} %get-tuple-element.6), channel_id=1, replica_groups=mesh['trow'=4,'tcol'=4,'pix'=16] {'trow','tcol'}, use_global_device_ids=true, to_apply=%region_1.2 | all-reduce | flops 1024 | bytes 8192 | tf_op jit(solution)/shard_map/psum | solution.py:44
  50.1 0.2 divide_reduce_fusion
  50.3 28.0 %psum.15 = f32[384,2]{0,1:T(2,128)S(1)} all-reduce(f32[384,2]{0,1:T(2,128)S(1)} %divide_reduce_fusion), channel_id=1, replica_groups=mesh['trow'=4,'tcol'=4,'pix'=16] {'pix'}, use_global_device_ids=true, to_apply=%region_3.4 | all-reduce | flops 768 | bytes 6144 | tf_op jit(solution)/shard_map/psum | solution.py:46
  78.3 1.2 copy_bitcast_fusion
  79.5 0.0 all-gather.2.cloned.1.call-update
  79.5 0.0 reduce-scatter.5.cloned.1.call-start
  79.6 99.5 %all-gather.2.cloned.1.call-done = bf16[6144,2,512]{2,0,1:T(8,128)(2,1)} async-done(((bf16[384,2,512]{2,0,1:T(8,128)(2,1)}), bf16[6144,2,512]{2,0,1:T(8,128)(2,1)}) %all-gather.2.cloned.1.call-update) | async-done | bytes 12582928 | tf_op jit(solution)/shard_map/all_gather | solution.py:50
  179.1 8.2 %fusion.4 = f32[1536,1536]{1,0:T(8,128)} fusion(bf16[6144,2,512]{2,0,1:T(8,128)(2,1)} %all-gather.2.cloned.1.call-done, s32[]{:T(128)S(6)} %select_n.7, s32[]{:T(128)S(6)} %add.38, s32[]{:T(128)S(6)} %select_n.6), kind=kOutput, calls=%fused_computation.7 | convolution fusion | flops 2415919104 | bytes 12584960 | tf_op jit(solution)/shard_map/dot_general | solution.py:64
  187.3 0.0 reduce-scatter.5.cloned.1.call-update
  187.3 0.0 reduce-scatter.3.cloned.1.call-start
  187.4 8.1 %fusion.5 = f32[1536,1536]{1,0:T(8,128)} fusion(bf16[6144,2,512]{2,0,1:T(8,128)(2,1)} %all-gather.2.cloned.1.call-done, s32[]{:T(128)S(6)} %select_n.7, s32[]{:T(128)S(6)} %select_n.6), kind=kOutput, calls=%fused_computation.10 | convolution fusion | flops 2415919104 | bytes 12582920 | tf_op jit(solution)/shard_map/dot_general | solution.py:64
  195.5 0.0 reduce-scatter.3.cloned.1.call-update
  195.5 64.3 %reduce-scatter.5.cloned.1.call-done = f32[96,1536]{1,0:T(8,128)} async-done(((f32[1536,1536]{1,0:T(8,128)}), f32[96,1536]{1,0:T(8,128)}) %reduce-scatter.5.cloned.1.call-update) | async-done | bytes 589840 | tf_op jit(solution)/shard_map/reduce_scatter | solution.py:68
  259.8 1.9 broadcast_multiply_fusion
  261.7 73.0 %reduce-scatter.3.cloned.1.call-done = f32[96,1536]{1,0:T(8,128)} async-done(((f32[1536,1536]{1,0:T(8,128)}), f32[96,1536]{1,0:T(8,128)}) %reduce-scatter.3.cloned.1.call-update) | async-done | bytes 589840 | tf_op jit(solution)/shard_map/reduce_scatter | solution.py:68
  334.7 1.9 broadcast_multiply_fusion.1
  (5 shorter events, 0.1 us)
Async XLA Ops:
  7.2 4.9 %copy-start = (s32[384,2]{0,1:T(2,128)S(1)}, s32[384,2]{0,1:T(2,128)}, u32[]{:S(2)}) copy-start(s32[384,2]{0,1:T(2,128)} %param.3) | copy-start | bytes 9220
  7.2 172.0 %all-gather.2.cloned.1.call-start = ((), (), s32[]{:S(2)}) async-start(), calls=%async_computation.2 | async-start | bytes 13369344 | tf_op jit(solution)/shard_map/all_gather | solution.py:50
  9.0 3.1 collective-permute-start
  10.7 5.0 %collective-permute-start.1 = (bf16[384,2,1,128]{3,0,2,1:T(8,128)(2,1)S(1)}, bf16[384,2,1,128]{3,0,2,1:T(8,128)(2,1)S(1)}, u32[]{:S(2)}, u32[]{:S(2)}) collective-permute-start(bf16[384,2,1,128]{3,0,2,1:T(8,128)(2,1)S(1)} %get-tuple-element.9), channel_id=1, source_target_pairs={{1,0},{2,1},{3,2},{4,3},{5,4},{6,5},{7,6},{8,7},{9,8},{10,9},{11,1... | collective-permute-start | bytes 589832 | tf_op jit(solution)/shard_map/ppermute | solution.py:17
  79.5 180.3 %reduce-scatter.5.cloned.1.call-start = ((), (), s32[]{:S(2)}) async-start(), calls=%async_computation.4 | async-start | bytes 10027008 | tf_op jit(solution)/shard_map/reduce_scatter | solution.py:68
  187.3 147.4 %reduce-scatter.3.cloned.1.call-start = ((), (), s32[]{:S(2)}) async-start(), calls=%async_computation.3 | async-start | bytes 10027008 | tf_op jit(solution)/shard_map/reduce_scatter | solution.py:68
Sparse Core Ops, SparseCore 0:
  79.7 99.4 all-gather.1
  187.5 72.3 reduce-scatter.4
  262.4 72.2 reduce-scatter.2
where the time goes:
time: 343 us
  waiting for transfers between devices  240 us (70%)
  blocking collectives  60.7 us (18%)
  matrix products  16.3 us (5%)
  between operations  13.8 us (4%)
  other arithmetic  6.9 us (2%)
    reduce_scatter x2, waiting for transfers between devices, per_device(): lax.psum_scatter(partial_gram(jnp.int32(0), lax.axis_size('pix') * own_ro...  137 us
    all_gather x1, waiting for transfers between devices, per_device(): everything = lax.all_gather(normed, ('trow', 'tcol'), axis=0, tiled=True)  99.5 us
    psum x1, blocking collectives, per_device(): lax.psum(jnp.sum(shifted, axis=0), ('trow', 'tcol')) / total_frames  32.7 us
    psum x1, blocking collectives, per_device(): frame_mean = lax.psum(jnp.sum(flat, axis=(2, 3)), 'pix') / band_pixels  28 us
    dot_general x2, matrix products, partial_gram(): lax.dot_general(band_rows, band_cols, (((1,), (1,)), ((), ())), preferred...  16.3 us
  transfers between devices with their start and end apart: 5, of which 4 were waited for; matrix products, arithmetic and copies ran while one was open for 3% of the time, Pallas kernels for 0%

commit v1 on v0

--- a/solution.py
+++ b/solution.py
@@ -2,6 +2,24 @@
 import jax.numpy as jnp
 from jax import lax
 from jax.sharding import PartitionSpec as P
+
+
+def collect(array, axis, dim):
+    ways, here, lap = (lax.axis_size(axis), lax.axis_index(axis), array.shape[dim])
+    lengths = [n * ways if d == dim else n for d, n in enumerate(array.shape)]
+    full = lax.dynamic_update_slice_in_dim(
+        jnp.zeros(lengths, array.dtype), array, here * lap, axis=dim
+    )
+    going_up = going_down = array
+    for far in range(1, ways // 2 + 1):
+        going_up = lax.ppermute(going_up, axis, [(d, (d + 1) % ways) for d in range(ways)])
+        full = lax.dynamic_update_slice_in_dim(full, going_up, (here - far) % ways * lap, axis=dim)
+        if 2 * far < ways:
+            going_down = lax.ppermute(going_down, axis, [(d, (d - 1) % ways) for d in range(ways)])
+            full = lax.dynamic_update_slice_in_dim(
+                full, going_down, (here + far) % ways * lap, axis=dim
+            )
+    return full
 
 
 def extended(cells, sides, width):
@@ -47,7 +65,7 @@
     normed = (flat / frame_mean[:, :, None, None]).astype(jnp.bfloat16)
     normed = normed.reshape(local_frames, 2, tile_rows * columns)
     block_size = local_frames * lax.axis_size("tcol")
-    everything = lax.all_gather(normed, ("trow", "tcol"), axis=0, tiled=True)
+    everything = collect(normed, ("trow", "tcol"), 0)
     row_frames = lax.dynamic_slice_in_dim(
         everything, lax.axis_index("trow") * block_size, block_size, 0
     )

time: 343 us -> 409 us (1.19)
  starting transfers between devices: 3.16 us -> 35.6 us
  local copies, waits for them, and re-layouts: 1.75 us -> 25.9 us
  waiting for transfers between devices: 240 us -> 245 us
    ppermute x0 -> x15, waiting for transfers between devices: none -> 101 us  [the longest x8 98.1 us: collect(): lax.ppermute(going_up, axis, [(d, (d + 1) % ways) for d in range(ways)])]
    all_gather x1 -> x0, waiting for transfers between devices: 99.5 us -> none  [per_device(): everything = lax.all_gather(normed, ('trow', 'tcol'), axis=0, tiled=True)]
    ppermute x0 -> x15, starting transfers between devices: none -> 31.2 us  [the longest x8 19.8 us: collect(): lax.ppermute(going_up, axis, [(d, (d + 1) % ways) for d in range(ways)])]
    dynamic_update_slice x0 -> x15, local copies, waits for them, and re-layouts: none -> 18.8 us  [the longest x8 9.89 us: collect(): lax.dynamic_update_slice_in_dim(full, going_up, (here - far) % ways * lap...]
    reduce_scatter x2, waiting for transfers between devices: 137 us -> 145 us  [per_device(): lax.psum_scatter(partial_gram(jnp.int32(0), lax.axis_size('pix') * own_ro...]
    broadcast_in_dim x0 -> x1, local copies, waits for them, and re-layouts: none -> 5.34 us  [collect(): jnp.zeros(lengths, array.dtype)]
  transfers between devices with their start and end apart: 5 -> 19, of which waited for: 4 -> 12; matrix products, arithmetic and copies ran while one was open for 3% -> 9% of each run, Pallas kernels for 0% -> 0%
where the time goes in v1:
time: 409 us; the launch traced here: 408 us
  waiting for transfers between devices  245 us (60%)
  blocking collectives  62.7 us (15%)
  starting transfers between devices  35.6 us (9%)
  local copies, waits for them, and re-layouts  25.9 us (6%)
  matrix products  16.3 us (4%)
  between operations  14.1 us (3%)
  other arithmetic  7.91 us (2%)
    reduce_scatter x2, waiting for transfers between devices, per_device(): lax.psum_scatter(partial_gram(jnp.int32(0), lax.axis_size('pix') * own_ro...  145 us
    ppermute x8, waiting for transfers between devices, collect(): lax.ppermute(going_up, axis, [(d, (d + 1) % ways) for d in range(ways)])  98.1 us
    psum x1, blocking collectives, per_device(): lax.psum(jnp.sum(shifted, axis=0), ('trow', 'tcol')) / total_frames  33.7 us
    psum x1, blocking collectives, per_device(): frame_mean = lax.psum(jnp.sum(flat, axis=(2, 3)), 'pix') / band_pixels  29 us
    ppermute x8, starting transfers between devices, collect(): lax.ppermute(going_up, axis, [(d, (d + 1) % ways) for d in range(ways)])  19.8 us
    dot_general x2, matrix products, partial_gram(): lax.dot_general(band_rows, band_cols, (((1,), (1,)), ((), ())), preferred...  16.3 us
    ppermute x7, starting transfers between devices, collect(): lax.ppermute(going_down, axis, [(d, (d - 1) % ways) for d in range(ways)])  11.4 us
    dynamic_update_slice x8, local copies, waits for them, and re-layouts, collect(): lax.dynamic_update_slice_in_dim(full, going_up, (here - far) % ways * lap...  9.89 us
  transfers between devices with their start and end apart: 19, of which 12 were waited for; matrix products, arithmetic and copies ran while one was open for 9% of the time, Pallas kernels for 0%

profile of v1, /device:TPU:6, one launch (start us, length us, event | category | flops | bytes accessed | tf_op | source)
XLA Modules:
  0.0 408.0 jit_solution(16572981332965644357)
XLA Ops:
  7.2 1.7 copy.12
  9.0 1.3 collective-permute-start.1
  10.3 3.0 collective-permute-start
  14.9 1.0 fusion.11
  16.0 33.7 %psum.14 = f32[2,4,128]{2,1,0:T(4,128)S(1)} all-reduce(f32[2,4,128]{2,1,0:T(4,128)S(1)} %get-tuple-element.6), channel_id=1, replica_groups=mesh['trow'=4,'tcol'=4,'pix'=16] {'trow','tcol'}, use_global_device_ids=true, to_apply=%region_1.2 | all-reduce | flops 1024 | bytes 8192 | tf_op jit(solution)/shard_map/psum | solution.py:62
  49.9 29.0 %psum.15 = f32[384,2]{0,1:T(2,128)S(1)} all-reduce(f32[384,2]{0,1:T(2,128)S(1)} %divide_reduce_fusion), channel_id=1, replica_groups=mesh['trow'=4,'tcol'=4,'pix'=16] {'pix'}, use_global_device_ids=true, to_apply=%region_3.4 | all-reduce | flops 768 | bytes 6144 | tf_op jit(solution)/shard_map/psum | solution.py:64
  79.2 3.4 collective-permute-start.2
  82.6 1.3 collective-permute-start.3
  83.9 18.0 %collective-permute-done.2 = bf16[384,2,512]{2,0,1:T(8,128)(2,1)S(1)} collective-permute-done((bf16[384,2,512]{2,0,1:T(8,128)(2,1)S(1)}, bf16[384,2,512]{2,0,1:T(8,128)(2,1)S(1)}, u32[]{:S(2)}, u32[]{:S(2)}) %collective-permute-start.2) | collective-permute-done | bytes 786464 | tf_op jit(solution)/shard_map/ppermute | solution.py:15
  101.8 2.6 collective-permute-start.4
  104.5 16.7 %collective-permute-done.4 = bf16[384,2,512]{2,0,1:T(8,128)(2,1)S(1)} collective-permute-done((bf16[384,2,512]{2,0,1:T(8,128)(2,1)S(1)}, bf16[384,2,512]{2,0,1:T(8,128)(2,1)S(1)}, u32[]{:S(2)}, u32[]{:S(2)}) %collective-permute-start.4) | collective-permute-done | bytes 786464 | tf_op jit(solution)/shard_map/ppermute | solution.py:15
  121.1 4.4 %collective-permute-start.6 = (bf16[384,2,512]{2,0,1:T(8,128)(2,1)S(1)}, bf16[384,2,512]{2,0,1:T(8,128)(2,1)S(1)}, u32[]{:S(2)}, u32[]{:S(2)}) collective-permute-start(bf16[384,2,512]{2,0,1:T(8,128)(2,1)S(1)} %collective-permute-done.4), channel_id=1, source_target_pairs={{0,16},{16,32},{32,48},{48,64},{64,80},{80,96},{96,112},{112,128},... | collective-permute-start | bytes 2359304 | tf_op jit(solution)/shard_map/ppermute | solution.py:15
  125.6 16.2 %collective-permute-done.6 = bf16[384,2,512]{2,0,1:T(8,128)(2,1)S(1)} collective-permute-done((bf16[384,2,512]{2,0,1:T(8,128)(2,1)S(1)}, bf16[384,2,512]{2,0,1:T(8,128)(2,1)S(1)}, u32[]{:S(2)}, u32[]{:S(2)}) %collective-permute-start.6) | collective-permute-done | bytes 786464 | tf_op jit(solution)/shard_map/ppermute | solution.py:15
  141.8 4.0 collective-permute-start.8
  145.8 1.3 collective-permute-start.9
  147.0 15.1 %collective-permute-done.8 = bf16[384,2,512]{2,0,1:T(8,128)(2,1)S(1)} collective-permute-done((bf16[384,2,512]{2,0,1:T(8,128)(2,1)S(1)}, bf16[384,2,512]{2,0,1:T(8,128)(2,1)S(1)}, u32[]{:S(2)}, u32[]{:S(2)}) %collective-permute-start.8) | collective-permute-done | bytes 786464 | tf_op jit(solution)/shard_map/ppermute | solution.py:15
  162.2 2.9 collective-permute-start.10
  165.0 2.5 collective-permute-start.11
  167.5 14.4 %collective-permute-done.10 = bf16[384,2,512]{2,0,1:T(8,128)(2,1)} collective-permute-done((bf16[384,2,512]{2,0,1:T(8,128)(2,1)S(1)}, bf16[384,2,512]{2,0,1:T(8,128)(2,1)}, u32[]{:S(2)}, u32[]{:S(2)}) %collective-permute-start.10) | collective-permute-done | bytes 786464 | tf_op jit(solution)/shard_map/ppermute | solution.py:15
  181.8 1.6 collective-permute-start.12
  183.5 5.3 %broadcast_in_dim.2 = bf16[6144,2,512]{2,0,1:T(8,128)(2,1)} broadcast(bf16[]{:T(256)} %constant.110.clone.1), dimensions={} | broadcast | bytes 12582914 | tf_op jit(solution)/shard_map/broadcast_in_dim | solution.py:11
  188.8 1.2 constant_dynamic-update-slice_fusion.15
  190.0 1.0 constant_dynamic-update-slice_fusion.14
  191.0 2.9 collective-permute-start.13
  193.9 1.0 constant_dynamic-update-slice_fusion.13
  194.8 6.0 %collective-permute-done.12 = bf16[384,2,512]{2,0,1:T(8,128)(2,1)} collective-permute-done((bf16[384,2,512]{2,0,1:T(8,128)(2,1)}, bf16[384,2,512]{2,0,1:T(8,128)(2,1)}, u32[]{:S(2)}, u32[]{:S(2)}) %collective-permute-start.12) | collective-permute-done | bytes 786464 | tf_op jit(solution)/shard_map/ppermute | solution.py:15
  201.2 1.0 constant_dynamic-update-slice_fusion.12
  202.2 1.0 constant_dynamic-update-slice_fusion.11
  203.1 1.0 constant_dynamic-update-slice_fusion.10
  204.1 1.0 constant_dynamic-update-slice_fusion.9
  205.1 0.9 constant_dynamic-update-slice_fusion.8
  206.0 2.5 collective-permute-done.13
  208.6 3.4 collective-permute-start.15
  212.0 2.1 constant_dynamic-update-slice_fusion.7
  214.1 4.5 %collective-permute-done.14 = bf16[384,2,512]{2,0,1:T(8,128)(2,1)S(1)} collective-permute-done((bf16[384,2,512]{2,0,1:T(8,128)(2,1)}, bf16[384,2,512]{2,0,1:T(8,128)(2,1)S(1)}, u32[]{:S(2)}, u32[]{:S(2)}) %collective-permute-start.14) | collective-permute-done | bytes 786464 | tf_op jit(solution)/shard_map/ppermute | solution.py:15
  219.1 2.1 constant_dynamic-update-slice_fusion.6
  221.2 2.1 constant_dynamic-update-slice_fusion.5
  223.3 2.1 constant_dynamic-update-slice_fusion.4
  226.3 0.9 constant_dynamic-update-slice_fusion.2
  227.2 0.9 constant_dynamic-update-slice_fusion.1
  228.2 7.3 %collective-permute-done.16 = bf16[384,2,512]{2,0,1:T(8,128)(2,1)S(1)} collective-permute-done((bf16[384,2,512]{2,0,1:T(8,128)(2,1)S(1)}, bf16[384,2,512]{2,0,1:T(8,128)(2,1)S(1)}, u32[]{:S(2)}, u32[]{:S(2)}) %collective-permute-start.16) | collective-permute-done | bytes 786464 | tf_op jit(solution)/shard_map/ppermute | solution.py:15
  235.4 1.0 constant_dynamic-update-slice_fusion
  236.4 8.1 %fusion.5 = f32[1536,1536]{1,0:T(8,128)} fusion(bf16[6144,2,512]{2,0,1:T(8,128)(2,1)} %constant_dynamic-update-slice_fusion, s32[]{:T(128)S(6)} %select_n.149, s32[]{:T(128)S(6)} %select_n.148), kind=kOutput, calls=%fused_computation.10 | convolution fusion | flops 2415919104 | bytes 12582920 | tf_op jit(solution)/shard_map/dot_general | solution.py:82
  244.6 8.2 %fusion.4 = f32[1536,1536]{1,0:T(8,128)} fusion(bf16[6144,2,512]{2,0,1:T(8,128)(2,1)} %constant_dynamic-update-slice_fusion, s32[]{:T(128)S(6)} %select_n.149, s32[]{:T(128)S(6)} %add.203, s32[]{:T(128)S(6)} %select_n.148), kind=kOutput, calls=%fused_computation.7 | convolution fusion | flops 2415919104 | bytes 12584960 | tf_op jit(solution)/shard_map/dot_general | solution.py:82
  252.8 72.0 %reduce-scatter.3.cloned.1.call-done = f32[96,1536]{1,0:T(8,128)} async-done(((f32[1536,1536]{1,0:T(8,128)}), f32[96,1536]{1,0:T(8,128)}) %reduce-scatter.3.cloned.1.call-update) | async-done | bytes 589840 | tf_op jit(solution)/shard_map/reduce_scatter | solution.py:86
  324.7 1.9 broadcast_multiply_fusion.1
  326.6 72.6 %reduce-scatter.5.cloned.1.call-done = f32[96,1536]{1,0:T(8,128)} async-done(((f32[1536,1536]{1,0:T(8,128)}), f32[96,1536]{1,0:T(8,128)}) %reduce-scatter.5.cloned.1.call-update) | async-done | bytes 589840 | tf_op jit(solution)/shard_map/reduce_scatter | solution.py:86
  399.3 1.9 broadcast_multiply_fusion
  (46 shorter events, 4.0 us)
Async XLA Ops:
  7.2 317.5 %reduce-scatter.3.cloned.1.call-start = ((), (), s32[]{:S(2)}) async-start(), calls=%async_computation.2 | async-start | bytes 10027008 | tf_op jit(solution)/shard_map/reduce_scatter | solution.py:86
  9.0 5.2 %collective-permute-start.1 = (bf16[384,2,1,128]{3,0,2,1:T(8,128)(2,1)S(1)}, bf16[384,2,1,128]{3,0,2,1:T(8,128)(2,1)S(1)}, u32[]{:S(2)}, u32[]{:S(2)}) collective-permute-start(bf16[384,2,1,128]{3,0,2,1:T(8,128)(2,1)S(1)} %get-tuple-element.9), channel_id=1, source_target_pairs={{1,0},{2,1},{3,2},{4,3},{5,4},{6,5},{7,6},{8,7},{9,8},{10,9},{11,1... | collective-permute-start | bytes 589832 | tf_op jit(solution)/shard_map/ppermute | solution.py:35
  10.3 4.1 %collective-permute-start = (bf16[384,2,1,128]{3,0,2,1:T(8,128)(2,1)S(1)}, bf16[384,2,1,128]{3,0,2,1:T(8,128)(2,1)S(1)}, u32[]{:S(2)}, u32[]{:S(2)}) collective-permute-start(bf16[384,2,1,128]{3,0,2,1:T(8,128)(2,1)S(1)} %get-tuple-element.8), channel_id=1, source_target_pairs={{0,1},{1,2},{2,3},{3,4},{4,5},{5,6},{6,7},{7,8},{8,9},{9,10},{10,1... | collective-permute-start | bytes 589832 | tf_op jit(solution)/shard_map/ppermute | solution.py:33
  79.2 22.6 %collective-permute-start.2 = (bf16[384,2,512]{2,0,1:T(8,128)(2,1)S(1)}, bf16[384,2,512]{2,0,1:T(8,128)(2,1)S(1)}, u32[]{:S(2)}, u32[]{:S(2)}) collective-permute-start(bf16[384,2,512]{2,0,1:T(8,128)(2,1)S(1)} %copy_bitcast_fusion), channel_id=1, source_target_pairs={{0,16},{16,32},{32,48},{48,64},{64,80},{80,96},{96,112},{112,128},... | collective-permute-start | bytes 2359304 | tf_op jit(solution)/shard_map/ppermute | solution.py:15
  82.6 21.9 %collective-permute-start.3 = (bf16[384,2,512]{2,0,1:T(8,128)(2,1)S(1)}, bf16[384,2,512]{2,0,1:T(8,128)(2,1)S(1)}, u32[]{:S(2)}, u32[]{:S(2)}) collective-permute-start(bf16[384,2,512]{2,0,1:T(8,128)(2,1)S(1)} %copy_bitcast_fusion), channel_id=1, source_target_pairs={{0,240},{16,0},{32,16},{48,32},{64,48},{80,64},{96,80},{112,96},{1... | collective-permute-start | bytes 2359304 | tf_op jit(solution)/shard_map/ppermute | solution.py:18
  101.8 2.6 copy-start.6
  101.8 19.3 %collective-permute-start.4 = (bf16[384,2,512]{2,0,1:T(8,128)(2,1)S(1)}, bf16[384,2,512]{2,0,1:T(8,128)(2,1)S(1)}, u32[]{:S(2)}, u32[]{:S(2)}) collective-permute-start(bf16[384,2,512]{2,0,1:T(8,128)(2,1)S(1)} %collective-permute-done.2), channel_id=1, source_target_pairs={{0,16},{16,32},{32,48},{48,64},{64,80},{80,96},{96,112},{112,128},... | collective-permute-start | bytes 2359304 | tf_op jit(solution)/shard_map/ppermute | solution.py:15
  104.5 21.1 %collective-permute-start.5 = (bf16[384,2,512]{2,0,1:T(8,128)(2,1)S(1)}, bf16[384,2,512]{2,0,1:T(8,128)(2,1)S(1)}, u32[]{:S(2)}, u32[]{:S(2)}) collective-permute-start(bf16[384,2,512]{2,0,1:T(8,128)(2,1)S(1)} %collective-permute-done.3), channel_id=1, source_target_pairs={{0,240},{16,0},{32,16},{48,32},{64,48},{80,64},{96,80},{112,96},{1... | collective-permute-start | bytes 2359304 | tf_op jit(solution)/shard_map/ppermute | solution.py:18
  121.1 20.6 %collective-permute-start.6 = (bf16[384,2,512]{2,0,1:T(8,128)(2,1)S(1)}, bf16[384,2,512]{2,0,1:T(8,128)(2,1)S(1)}, u32[]{:S(2)}, u32[]{:S(2)}) collective-permute-start(bf16[384,2,512]{2,0,1:T(8,128)(2,1)S(1)} %collective-permute-done.4), channel_id=1, source_target_pairs={{0,16},{16,32},{32,48},{48,64},{64,80},{80,96},{96,112},{112,128},... | collective-permute-start | bytes 2359304 | tf_op jit(solution)/shard_map/ppermute | solution.py:15
  125.6 16.2 %copy-start = (bf16[384,2,512]{2,0,1:T(8,128)(2,1)}, bf16[384,2,512]{2,0,1:T(8,128)(2,1)S(1)}, u32[]{:S(2)}) copy-start(bf16[384,2,512]{2,0,1:T(8,128)(2,1)S(1)} %collective-permute-done.5) | copy-start | bytes 2359300
  125.6 20.2 %collective-permute-start.7 = (bf16[384,2,512]{2,0,1:T(8,128)(2,1)S(1)}, bf16[384,2,512]{2,0,1:T(8,128)(2,1)S(1)}, u32[]{:S(2)}, u32[]{:S(2)}) collective-permute-start(bf16[384,2,512]{2,0,1:T(8,128)(2,1)S(1)} %collective-permute-done.5), channel_id=1, source_target_pairs={{0,240},{16,0},{32,16},{48,32},{64,48},{80,64},{96,80},{112,96},{1... | collective-permute-start | bytes 2359304 | tf_op jit(solution)/shard_map/ppermute | solution.py:18
  141.8 4.0 copy-start.2
  141.8 20.4 %collective-permute-start.8 = (bf16[384,2,512]{2,0,1:T(8,128)(2,1)S(1)}, bf16[384,2,512]{2,0,1:T(8,128)(2,1)S(1)}, u32[]{:S(2)}, u32[]{:S(2)}) collective-permute-start(bf16[384,2,512]{2,0,1:T(8,128)(2,1)S(1)} %collective-permute-done.6), channel_id=1, source_target_pairs={{0,16},{16,32},{32,48},{48,64},{64,80},{80,96},{96,112},{112,128},... | collective-permute-start | bytes 2359304 | tf_op jit(solution)/shard_map/ppermute | solution.py:15
  145.8 16.4 %copy-start.4 = (bf16[384,2,512]{2,0,1:T(8,128)(2,1)}, bf16[384,2,512]{2,0,1:T(8,128)(2,1)S(1)}, u32[]{:S(2)}) copy-start(bf16[384,2,512]{2,0,1:T(8,128)(2,1)S(1)} %collective-permute-done.7) | copy-start | bytes 2359300
  145.8 19.3 %collective-permute-start.9 = (bf16[384,2,512]{2,0,1:T(8,128)(2,1)S(1)}, bf16[384,2,512]{2,0,1:T(8,128)(2,1)}, u32[]{:S(2)}, u32[]{:S(2)}) collective-permute-start(bf16[384,2,512]{2,0,1:T(8,128)(2,1)S(1)} %collective-permute-done.7), channel_id=1, source_target_pairs={{0,240},{16,0},{32,16},{48,32},{64,48},{80,64},{96,80},{112,96},{1... | collective-permute-start | bytes 2359304 | tf_op jit(solution)/shard_map/ppermute | solution.py:18
  162.2 2.9 copy-start.8
  162.2 19.7 %collective-permute-start.10 = (bf16[384,2,512]{2,0,1:T(8,128)(2,1)S(1)}, bf16[384,2,512]{2,0,1:T(8,128)(2,1)}, u32[]{:S(2)}, u32[]{:S(2)}) collective-permute-start(bf16[384,2,512]{2,0,1:T(8,128)(2,1)S(1)} %collective-permute-done.8), channel_id=1, source_target_pairs={{0,16},{16,32},{32,48},{48,64},{64,80},{80,96},{96,112},{112,128},... | collective-permute-start | bytes 2359304 | tf_op jit(solution)/shard_map/ppermute | solution.py:15
  165.0 25.9 %collective-permute-start.11 = (bf16[384,2,512]{2,0,1:T(8,128)(2,1)}, bf16[384,2,512]{2,0,1:T(8,128)(2,1)}, u32[]{:S(2)}, u32[]{:S(2)}) collective-permute-start(bf16[384,2,512]{2,0,1:T(8,128)(2,1)} %collective-permute-done.9), channel_id=1, source_target_pairs={{0,240},{16,0},{32,16},{48,32},{64,48},{80,64},{96,80},{112,96},{1... | collective-permute-start | bytes 2359304 | tf_op jit(solution)/shard_map/ppermute | solution.py:18
  181.8 19.0 %collective-permute-start.12 = (bf16[384,2,512]{2,0,1:T(8,128)(2,1)}, bf16[384,2,512]{2,0,1:T(8,128)(2,1)}, u32[]{:S(2)}, u32[]{:S(2)}) collective-permute-start(bf16[384,2,512]{2,0,1:T(8,128)(2,1)} %collective-permute-done.10), channel_id=1, source_target_pairs={{0,16},{16,32},{32,48},{48,64},{64,80},{80,96},{96,112},{112,128},... | collective-permute-start | bytes 2359304 | tf_op jit(solution)/shard_map/ppermute | solution.py:15
  183.5 6.5 %copy-start.7 = (bf16[384,2,512]{2,0,1:T(8,128)(2,1)S(1)}, bf16[384,2,512]{2,0,1:T(8,128)(2,1)}, u32[]{:S(2)}) copy-start(bf16[384,2,512]{2,0,1:T(8,128)(2,1)} %copy-done.6) | copy-start | bytes 2359300
  183.5 18.7 %copy-start.1 = (bf16[384,2,512]{2,0,1:T(8,128)(2,1)S(1)}, bf16[384,2,512]{2,0,1:T(8,128)(2,1)}, u32[]{:S(2)}) copy-start(bf16[384,2,512]{2,0,1:T(8,128)(2,1)} %copy-done) | copy-start | bytes 2359300
  183.5 19.7 %copy-start.3 = (bf16[384,2,512]{2,0,1:T(8,128)(2,1)S(1)}, bf16[384,2,512]{2,0,1:T(8,128)(2,1)}, u32[]{:S(2)}) copy-start(bf16[384,2,512]{2,0,1:T(8,128)(2,1)} %copy-done.2) | copy-start | bytes 2359300
  183.5 20.6 %copy-start.5 = (bf16[384,2,512]{2,0,1:T(8,128)(2,1)S(1)}, bf16[384,2,512]{2,0,1:T(8,128)(2,1)}, u32[]{:S(2)}) copy-start(bf16[384,2,512]{2,0,1:T(8,128)(2,1)} %copy-done.4) | copy-start | bytes 2359300
  188.8 16.2 %copy-start.9 = (bf16[384,2,512]{2,0,1:T(8,128)(2,1)S(1)}, bf16[384,2,512]{2,0,1:T(8,128)(2,1)}, u32[]{:S(2)}) copy-start(bf16[384,2,512]{2,0,1:T(8,128)(2,1)} %copy-done.8) | copy-start | bytes 2359300
  191.0 17.6 %collective-permute-start.13 = (bf16[384,2,512]{2,0,1:T(8,128)(2,1)}, bf16[384,2,512]{2,0,1:T(8,128)(2,1)S(1)}, u32[]{:S(2)}, u32[]{:S(2)}) collective-permute-start(bf16[384,2,512]{2,0,1:T(8,128)(2,1)} %collective-permute-done.11), channel_id=1, source_target_pairs={{0,240},{16,0},{32,16},{48,32},{64,48},{80,64},{96,80},{112,96},{1... | collective-permute-start | bytes 2359304 | tf_op jit(solution)/shard_map/ppermute | solution.py:18
  200.9 17.7 %collective-permute-start.14 = (bf16[384,2,512]{2,0,1:T(8,128)(2,1)}, bf16[384,2,512]{2,0,1:T(8,128)(2,1)S(1)}, u32[]{:S(2)}, u32[]{:S(2)}) collective-permute-start(bf16[384,2,512]{2,0,1:T(8,128)(2,1)} %collective-permute-done.12), channel_id=1, source_target_pairs={{0,16},{16,32},{32,48},{48,64},{64,80},{80,96},{96,112},{112,128},... | collective-permute-start | bytes 2359304 | tf_op jit(solution)/shard_map/ppermute | solution.py:15
  208.6 18.6 %collective-permute-start.15 = (bf16[384,2,512]{2,0,1:T(8,128)(2,1)S(1)}, bf16[384,2,512]{2,0,1:T(8,128)(2,1)S(1)}, u32[]{:S(2)}, u32[]{:S(2)}) collective-permute-start(bf16[384,2,512]{2,0,1:T(8,128)(2,1)S(1)} %collective-permute-done.13), channel_id=1, source_target_pairs={{0,240},{16,0},{32,16},{48,32},{64,48},{80,64},{96,80},{112,96},{1... | collective-permute-start | bytes 2359304 | tf_op jit(solution)/shard_map/ppermute | solution.py:18
  218.6 16.9 %collective-permute-start.16 = (bf16[384,2,512]{2,0,1:T(8,128)(2,1)S(1)}, bf16[384,2,512]{2,0,1:T(8,128)(2,1)S(1)}, u32[]{:S(2)}, u32[]{:S(2)}) collective-permute-start(bf16[384,2,512]{2,0,1:T(8,128)(2,1)S(1)} %collective-permute-done.14), channel_id=1, source_target_pairs={{0,16},{16,32},{32,48},{48,64},{64,80},{80,96},{96,112},{112,128},... | collective-permute-start | bytes 2359304 | tf_op jit(solution)/shard_map/ppermute | solution.py:15
  244.5 154.8 %reduce-scatter.5.cloned.1.call-start = ((), (), s32[]{:S(2)}) async-start(), calls=%async_computation.3 | async-start | bytes 10027008 | tf_op jit(solution)/shard_map/reduce_scatter | solution.py:86
Sparse Core Ops, SparseCore 0:
  244.6 80.0 reduce-scatter.2
  327.3 71.9 reduce-scatter.4
